TPU v7x, 32 devices: a whole 2x2x4 slice. The times are simulated.
32 devices in a mesh: row: 8 (over y, x, core), col: 4 (over z).
Axes of the slice: x: 2, y: 2, z: 4, core: 2. Of those that a mesh axis runs over, the one named last changes fastest.
Arguments:
- coeffs: bfloat16 [16384, 2048], P('row', 'col'), may hold values from -0.8984375 to 0.8984375
- occupations: float32 [2048], replicated, may hold values from 0.05 to 2
- block_order: int32 [32], replicated, may hold values from 0 to 31, as said below
- neighbours: int32 [32, 15], P(('row', 'col')), may hold values from 0 to 31, as said below
- counts: int32 [32], P(('row', 'col')), may hold values from 4 to 15, as said below
Outputs:
- density: bfloat16 [32, 15, 512, 512], P(('row', 'col'))
Inputs may be any that keep to these rules, and one draw needn't show every extreme that they name: Within each aligned group of 4 entries, block_order is a permutation of that group's own indices. For atom row block a, the first counts[a] entries of neighbours[a] are distinct blocks b with |b - a| < 8; the remaining entries equal a. `counts`: some block has 15 live slots in every draw.
All inputs are finite; a program needn't handle non-finite values.
Results may differ from a plain program's by a relative error of at most 0.0044.
Values may be sent and summed in bfloat16 or wider, within the bound.
A program may use at most 128 MiB of HBM per device.

v0:
```python
import jax
import jax.numpy as jnp
from jax import lax
from jax.sharding import PartitionSpec as P

W = 8
NNB = 15


def from_behind(block, axis, distance):
    devices = range(lax.axis_size(axis))
    route = [(i - distance, i) for i in devices if i - distance in devices]
    return lax.ppermute(block, axis, route)


def shards(coeffs, occupations, block_order, neighbours, counts):
    col_count = lax.axis_size("col")
    states_local = coeffs.shape[1]
    block_rows = coeffs.shape[0] // col_count
    group_base = lax.axis_index("row") * col_count
    own_index = group_base + lax.axis_index("col")
    local_blocks = coeffs.reshape(col_count, block_rows, states_local)
    picks = lax.dynamic_slice_in_dim(block_order, group_base, col_count) - group_base
    outgoing = local_blocks[picks]
    own_block = lax.all_to_all(outgoing, "col", split_axis=0, concat_axis=2, tiled=True)
    downward = own_block
    step = 1
    while step < W:
        received = from_behind(downward, ("row", "col"), step)
        downward = jnp.concatenate([downward, received], axis=0)
        step = step * 2
    upward = own_block
    step = 1
    while step < W:
        received = from_behind(upward, ("row", "col"), -step)
        upward = jnp.concatenate([upward, received], axis=0)
        step = step * 2
    window = jnp.concatenate([downward[1:][::-1], upward], axis=0)
    weighted = (own_block[0].astype(jnp.float32) * occupations[None, :]).astype(jnp.bfloat16)
    offsets = neighbours[0] - own_index + (W - 1)
    live_count = counts[0]
    chosen = window[offsets]
    products = jnp.einsum("ik,jnk->jin", weighted, chosen, preferred_element_type=jnp.float32)
    slots = jnp.arange(NNB, dtype=jnp.int32)
    live = (slots < live_count)[:, None, None]
    result = jnp.where(live, products, 0.0).astype(jnp.bfloat16)
    return result[None]


def solution(mesh):
    return jax.shard_map(
        shards,
        mesh=mesh,
        in_specs=(P("row", "col"), P(), P(), P(("row", "col"), None), P(("row", "col"))),
        out_specs=P(("row", "col"), None, None, None),
        check_vma=False,
    )
```

profile of v0, /device:TPU:20, one launch (start us, length us, event | category | flops | bytes accessed | tf_op | source)
XLA Modules:
  0.0 816.8 jit_solution(5868224025195781986)
XLA Ops:
  0.0 0.0 copy-start
  0.0 0.9 compare_select_fusion.1
  0.9 0.7 copy-done
  1.6 2.0 gather_fusion
  3.6 50.8 %all_to_all.18 = bf16[4,512,512]{2,1,0:T(8,128)(2,1)S(1)} all-to-all(bf16[4,512,512]{2,1,0:T(8,128)(2,1)} %gather_fusion), channel_id=1, replica_groups=mesh['row'=8,'col'=4] {'col'}, dimensions={0} | all-to-all | bytes 4194304 | tf_op jit(solution)/shard_map/all_to_all | solution.py:25
  54.4 0.0 copy-start.2
  54.4 2.7 copy.19
  57.1 0.0 copy-done.2
  57.1 2.9 copy.20
  60.0 3.7 collective-permute-start
  63.8 2.1 collective-permute-start.3
  65.9 44.5 %collective-permute-done = bf16[1,512,2048]{2,1,0:T(8,128)(2,1)S(1)} collective-permute-done((bf16[1,512,2048]{2,1,0:T(8,128)(2,1)S(1)}, bf16[1,512,2048]{2,1,0:T(8,128)(2,1)S(1)}, u32[]{:S(2)}, u32[]{:S(2)}) %collective-permute-start) | collective-permute-done | bytes 2097184 | tf_op jit(solution)/shard_map/ppermute | solution.py:13
  110.3 0.0 copy-start.3
  110.3 44.4 %collective-permute-done.3 = bf16[1,512,2048]{2,1,0:T(8,128)(2,1)S(1)} collective-permute-done((bf16[1,512,2048]{2,1,0:T(8,128)(2,1)S(1)}, bf16[1,512,2048]{2,1,0:T(8,128)(2,1)S(1)}, u32[]{:S(2)}, u32[]{:S(2)}) %collective-permute-start.3) | collective-permute-done | bytes 2097184 | tf_op jit(solution)/shard_map/ppermute | solution.py:13
  154.7 0.0 copy-start.4
  154.7 0.7 pad_maximum_fusion.3
  155.4 4.0 collective-permute-start.1
  159.4 0.0 copy-start.11
  159.4 2.7 collective-permute-start.4
  162.2 266.4 %collective-permute-done.1 = bf16[2,512,2048]{2,1,0:T(8,128)(2,1)S(1)} collective-permute-done((bf16[2,512,2048]{2,1,0:T(8,128)(2,1)S(1)}, bf16[2,512,2048]{2,1,0:T(8,128)(2,1)S(1)}, u32[]{:S(2)}, u32[]{:S(2)}) %collective-permute-start.1) | collective-permute-done | bytes 4194336 | tf_op jit(solution)/shard_map/ppermute | solution.py:13
  428.6 0.0 copy-start.6
  428.6 89.5 %collective-permute-done.4 = bf16[2,512,2048]{2,1,0:T(8,128)(2,1)S(1)} collective-permute-done((bf16[2,512,2048]{2,1,0:T(8,128)(2,1)S(1)}, bf16[2,512,2048]{2,1,0:T(8,128)(2,1)S(1)}, u32[]{:S(2)}, u32[]{:S(2)}) %collective-permute-start.4) | collective-permute-done | bytes 4194336 | tf_op jit(solution)/shard_map/ppermute | solution.py:13
  518.1 0.0 copy-start.8
  518.1 6.8 fusion.7
  524.9 0.0 copy-done.3
  524.9 0.0 copy-done.4
  524.9 0.0 copy-done.6
  524.9 0.3 copy-done.8
  525.2 0.0 copy-start.10
  525.2 2.0 collective-permute-start.2
  527.2 5.2 collective-permute-start.5
  533.1 0.0 copy-done.11
  533.1 4.1 bitcast_convert_fusion
  537.2 5.3 copy.27
  542.5 0.0 copy-done.10
  542.5 0.0 copy-start.7
  542.5 4.0 fusion.11
  546.5 161.8 %collective-permute-done.2 = bf16[4,512,2048]{2,1,0:T(8,128)(2,1)} collective-permute-done((bf16[4,512,2048]{2,1,0:T(8,128)(2,1)}, bf16[4,512,2048]{2,1,0:T(8,128)(2,1)}, u32[]{:S(2)}, u32[]{:S(2)}) %collective-permute-start.2) | collective-permute-done | bytes 8388640 | tf_op jit(solution)/shard_map/ppermute | solution.py:13
  708.4 0.0 copy-done.7
  708.4 6.4 pad_maximum_fusion
  714.8 0.0 copy-start.5
  714.8 6.0 reverse_dynamic-update-slice_fusion
  720.8 0.0 copy-start.9
  720.8 1.6 constant_dynamic-update-slice_fusion.3
  722.4 0.0 copy-done.5
  722.4 1.5 constant_dynamic-update-slice_fusion.2
  723.8 0.7 copy-done.9
  724.5 2.3 constant_dynamic-update-slice_fusion.1
  726.9 0.0 collective-permute-done.5
  726.9 8.4 %constant_dynamic-update-slice_fusion = bf16[15,512,2048]{2,1,0:T(8,128)(2,1)} fusion(bf16[15,512,2048]{2,1,0:T(8,128)(2,1)} %constant_dynamic-update-slice_fusion.1, bf16[4,512,2048]{2,1,0:T(8,128)(2,1)} %collective-permute-done.5), kind=kLoop, calls=%fused_computation.20 | loop fusion | bytes 16777216 | tf_op jit(solution)/shard_map/concatenate | solution.py:38
  735.2 23.1 %fusion.15 = (bf16[15,512,1024]{2,1,0:T(8,128)(2,1)}, bf16[15,512,1024]{2,1,0:T(8,128)(2,1)}) fusion(bf16[15,512,2048]{2,1,0:T(8,128)(2,1)} %constant_dynamic-update-slice_fusion), kind=kLoop, calls=%fused_computation.32 | loop fusion | bytes 62914560 | tf_op jit(solution)/shard_map/gather | solution.py:42
  758.3 12.3 %gather_fusion.1 = bf16[15,512,1024]{2,1,0:T(8,128)(2,1)} fusion(bf16[15,512,1024]{2,1,0:T(8,128)(2,1)} %get-tuple-element.5, s32[1024]{0:T(1024)S(1)} %pad_clamp_fusion), kind=kCustom, calls=%fused_computation.1 | custom fusion | bytes 31457340 | tf_op jit(solution)/shard_map/gather | solution.py:42
  770.7 12.4 %gather_fusion.2 = bf16[15,512,1024]{2,1,0:T(8,128)(2,1)} fusion(bf16[15,512,1024]{2,1,0:T(8,128)(2,1)} %get-tuple-element.6, s32[1024]{0:T(1024)S(1)} %pad_clamp_fusion), kind=kCustom, calls=%fused_computation.2 | custom fusion | bytes 31457340 | tf_op jit(solution)/shard_map/gather | solution.py:42
  783.1 0.0 copy-start.1
  783.1 23.1 %fusion.8 = bf16[1,15,512,512]{2,3,1,0:T(8,128)(2,1)} fusion(bf16[15,512,1024]{2,1,0:T(8,128)(2,1)} %gather_fusion.2, bf16[15,512,1024]{2,1,0:T(8,128)(2,1)} %gather_fusion.1, pred[15]{0:T(512)(128)(4,1)S(1)} %iota_compare_fusion, bf16[512,2048]{0,1:T(8,128)(2,1)} %fusion.11), kind=kOutput, calls=%fused_computation.14 | convolution fusion | flops 16176906240 | bytes 41418768 | tf_op jit(solution)/shard_map/ik,jnk->jin/dot_general | solution.py:43
  806.2 10.6 %copy.29 = bf16[1,15,512,512]{3,2,1,0:T(8,128)(2,1)} copy(bf16[1,15,512,512]{2,3,1,0:T(8,128)(2,1)} %fusion.8) | data formatting | bytes 15728640 | tf_op jit(solution)/shard_map/broadcast_in_dim | solution.py:47
  816.8 0.0 copy-done.1
  (4 shorter events, 0.0 us)
Async XLA Ops:
  0.0 1.6 copy-start
  54.4 2.7 copy-start.2
  60.0 50.3 %collective-permute-start = (bf16[1,512,2048]{2,1,0:T(8,128)(2,1)S(1)}, bf16[1,512,2048]{2,1,0:T(8,128)(2,1)S(1)}, u32[]{:S(2)}, u32[]{:S(2)}) collective-permute-start(bf16[1,512,2048]{2,1,0:T(8,128)(2,1)S(1)} %copy.20), channel_id=1, source_target_pairs={{0,1},{1,2},{2,3},{3,4},{4,5},{5,6},{6,7},{7,8},{8,9},{9,10},{10,1... | collective-permute-start | bytes 6291464 | tf_op jit(solution)/shard_map/ppermute | solution.py:13
  63.8 91.0 %collective-permute-start.3 = (bf16[1,512,2048]{2,1,0:T(8,128)(2,1)S(1)}, bf16[1,512,2048]{2,1,0:T(8,128)(2,1)S(1)}, u32[]{:S(2)}, u32[]{:S(2)}) collective-permute-start(bf16[1,512,2048]{2,1,0:T(8,128)(2,1)S(1)} %copy.20), channel_id=1, source_target_pairs={{1,0},{2,1},{3,2},{4,3},{5,4},{6,5},{7,6},{8,7},{9,8},{10,9},{11,1... | collective-permute-start | bytes 6291464 | tf_op jit(solution)/shard_map/ppermute | solution.py:13
  110.3 414.6 %copy-start.3 = (bf16[1,512,2048]{2,1,0:T(8,128)(2,1)}, bf16[1,512,2048]{2,1,0:T(8,128)(2,1)S(1)}, u32[]{:S(2)}) copy-start(bf16[1,512,2048]{2,1,0:T(8,128)(2,1)S(1)} %collective-permute-done) | copy-start | bytes 6291460
  154.7 370.2 %copy-start.4 = (bf16[1,512,2048]{2,1,0:T(8,128)(2,1)}, bf16[1,512,2048]{2,1,0:T(8,128)(2,1)S(1)}, u32[]{:S(2)}) copy-start(bf16[1,512,2048]{2,1,0:T(8,128)(2,1)S(1)} %collective-permute-done.3) | copy-start | bytes 6291460
  155.4 273.2 %collective-permute-start.1 = (bf16[2,512,2048]{2,1,0:T(8,128)(2,1)S(1)}, bf16[2,512,2048]{2,1,0:T(8,128)(2,1)S(1)}, u32[]{:S(2)}, u32[]{:S(2)}) collective-permute-start(bf16[2,512,2048]{2,1,0:T(8,128)(2,1)S(1)} %get-tuple-element.10), channel_id=1, source_target_pairs={{0,2},{1,3},{2,4},{3,5},{4,6},{5,7},{6,8},{7,9},{8,10},{9,11},{10,... | collective-permute-start | bytes 12582920 | tf_op jit(solution)/shard_map/ppermute | solution.py:13
  159.4 373.6 %copy-start.11 = (s32[1,15]{1,0:T(1,128)S(1)}, s32[1,15]{1,0:T(1,128)}, u32[]{:S(2)}) copy-start(s32[1,15]{1,0:T(1,128)} %param.8) | copy-start | bytes 184
  159.4 358.7 %collective-permute-start.4 = (bf16[2,512,2048]{2,1,0:T(8,128)(2,1)S(1)}, bf16[2,512,2048]{2,1,0:T(8,128)(2,1)S(1)}, u32[]{:S(2)}, u32[]{:S(2)}) collective-permute-start(bf16[2,512,2048]{2,1,0:T(8,128)(2,1)S(1)} %get-tuple-element.9), channel_id=1, source_target_pairs={{2,0},{3,1},{4,2},{5,3},{6,4},{7,5},{8,6},{9,7},{10,8},{11,9},{12,... | collective-permute-start | bytes 12582920 | tf_op jit(solution)/shard_map/ppermute | solution.py:13
  428.6 96.4 %copy-start.6 = (bf16[2,512,2048]{2,1,0:T(8,128)(2,1)}, bf16[2,512,2048]{2,1,0:T(8,128)(2,1)S(1)}, u32[]{:S(2)}) copy-start(bf16[2,512,2048]{2,1,0:T(8,128)(2,1)S(1)} %collective-permute-done.1) | copy-start | bytes 12582916
  518.1 7.1 copy-start.8
  525.2 17.3 %copy-start.10 = (f32[2048]{0:T(1024)S(1)}, f32[2048]{0:T(1024)}, u32[]{:S(2)}) copy-start(f32[2048]{0:T(1024)} %param.6) | copy-start | bytes 24580
  525.2 183.2 %collective-permute-start.2 = (bf16[4,512,2048]{2,1,0:T(8,128)(2,1)}, bf16[4,512,2048]{2,1,0:T(8,128)(2,1)}, u32[]{:S(2)}, u32[]{:S(2)}) collective-permute-start(bf16[4,512,2048]{2,1,0:T(8,128)(2,1)} %get-tuple-element.8), channel_id=1, source_target_pairs={{0,4},{1,5},{2,6},{3,7},{4,8},{5,9},{6,10},{7,11},{8,12},{9,13},{1... | collective-permute-start | bytes 25165832 | tf_op jit(solution)/shard_map/ppermute | solution.py:13
  527.2 199.6 %collective-permute-start.5 = (bf16[4,512,2048]{2,1,0:T(8,128)(2,1)}, bf16[4,512,2048]{2,1,0:T(8,128)(2,1)}, u32[]{:S(2)}, u32[]{:S(2)}) collective-permute-start(bf16[4,512,2048]{2,1,0:T(8,128)(2,1)} %get-tuple-element.7), channel_id=1, source_target_pairs={{4,0},{5,1},{6,2},{7,3},{8,4},{9,5},{10,6},{11,7},{12,8},{13,9},{1... | collective-permute-start | bytes 25165832 | tf_op jit(solution)/shard_map/ppermute | solution.py:13
  542.5 165.8 %copy-start.7 = (bf16[2,512,2048]{2,1,0:T(8,128)(2,1)S(1)}, bf16[2,512,2048]{2,1,0:T(8,128)(2,1)}, u32[]{:S(2)}) copy-start(bf16[2,512,2048]{2,1,0:T(8,128)(2,1)} %copy-done.6) | copy-start | bytes 12582916
  714.8 7.6 copy-start.5
  720.8 3.7 copy-start.9
  783.1 33.8 %copy-start.1 = (bf16[2048,512]{1,0:T(8,128)(2,1)S(1)}, bf16[2048,512]{1,0:T(8,128)(2,1)}, u32[]{:S(2)}) copy-start(bf16[2048,512]{1,0:T(8,128)(2,1)} %param.5) | copy-start | bytes 6291460
where the time goes:
time: 821 us; the launch traced here: 817 us
  waiting for transfers between devices  607 us (74%)
  local copies, waits for them, and re-layouts  92.7 us (11%)
  blocking collectives  50.8 us (6%)
  matrix products  23.1 us (3%)
  other arithmetic  22.9 us (3%)
  starting transfers between devices  19.8 us (2%)
    ppermute x6, waiting for transfers between devices, from_behind(): return lax.ppermute(block, axis, route)  607 us
    all_to_all x1, blocking collectives, shards(): lax.all_to_all(outgoing, 'col', split_axis=0, concat_axis=2, tiled=True)  50.8 us
    gather x3, local copies, waits for them, and re-layouts, shards(): chosen = window[offsets]  47.8 us
    dot_general x1, matrix products, shards(): jnp.einsum('ik,jnk->jin', weighted, chosen, preferred_element_type=jnp.fl...  23.1 us
    ppermute x6, starting transfers between devices, from_behind(): return lax.ppermute(block, axis, route)  19.8 us
  transfers between devices with their start and end apart: 6, of which 5 were waited for; matrix products, arithmetic and copies ran while one was open for 4% of the time, Pallas kernels for 0%

commit v1 on v0

v1 whole, which is shorter than its diff:
```python
import functools

import jax
import jax.numpy as jnp
from jax import lax
from jax.experimental import pallas as pl
from jax.experimental.pallas import tpu as pltpu
from jax.sharding import PartitionSpec as P

W = 8
MESH = pl.DeviceIdType.MESH


def kernel(rows, cols, per, own_ref, occ_ref, out_ref, gat, wgt, res, in_sem, dsem, fsem, psem, rsem, xsem, usem, osem, qsem):
    row, z = lax.axis_index("row"), lax.axis_index("col")
    k = lax.rem(row, per)
    base = row - k
    place = k * cols + z
    size = per * cols
    has_up, has_down = row + per < rows, row >= per

    def remote(src, dst, send, recv, device):
        return pltpu.make_async_remote_copy(
            src_ref=src, dst_ref=dst, send_sem=send, recv_sem=recv, device_id=device, device_id_type=MESH
        )

    def direct(i):
        return remote(gat.at[k, i, z], gat.at[k, i, z], dsem.at[i], rsem.at[k, i, z], (row, i))

    def onward(way, i, c):
        step = 1 - 2 * way
        there = lax.rem(z + step + cols, cols)
        return remote(gat.at[k, i, c], gat.at[k, i, c], fsem.at[way, i, c], rsem.at[k, i, c], (row, there))

    def partner(d, i, c):
        there = base + lax.rem(k + d, per)
        return remote(gat.at[k, i, c], gat.at[k, i, c], psem.at[d - 1, i, c], rsem.at[k, i, c], (there, z))

    def ship(way, c):
        there = lax.rem(row + (1 - 2 * way) * per + rows, rows)
        return remote(gat.at[k, z, c], wgt.at[way, c], xsem.at[way, c], usem.at[way, c], (there, z))

    def arrive(kk, i, c):
        remote(gat.at[kk, i, c], gat.at[kk, i, c], dsem.at[0], rsem.at[kk, i, c], (row, z)).wait_recv()

    def pass_on(i, c, act):
        @pl.when((c <= z) & (z < cols - 1) & (i != z + 1))
        def _():
            act(onward(0, i, c))

        @pl.when((c >= z) & (z > 0) & (i != z - 1))
        def _():
            act(onward(1, i, c))

        for d in range(1, per):
            act(partner(d, i, c))

    def ship_on(c, act):
        @pl.when(has_up)
        def _():
            act(ship(0, c))

        @pl.when(has_down)
        def _():
            act(ship(1, c))

    def start(copy):
        copy.start()

    def sent(copy):
        copy.wait_send()

    fill = pltpu.make_async_copy(own_ref, gat.at[k, :, z], in_sem)
    fill.start()
    barrier = pltpu.get_barrier_semaphore()
    for d in range(1, cols):
        pl.semaphore_signal(barrier, inc=1, device_id=(row, lax.rem(z + d, cols)), device_id_type=MESH)
    for d in range(1, per):
        pl.semaphore_signal(barrier, inc=1, device_id=(base + lax.rem(k + d, per), z), device_id_type=MESH)

    @pl.when(has_up)
    def _():
        pl.semaphore_signal(barrier, inc=1, device_id=(lax.rem(row + per, rows), z), device_id_type=MESH)

    @pl.when(has_down)
    def _():
        pl.semaphore_signal(barrier, inc=1, device_id=(lax.rem(row - per + rows, rows), z), device_id_type=MESH)

    pl.semaphore_wait(barrier, cols + per - 2 + has_up.astype(jnp.int32) + has_down.astype(jnp.int32))
    fill.wait()

    for d in range(1, cols):
        direct(lax.rem(z + d, cols)).start()
    ship_on(z, start)

    @pl.loop(0, cols)
    def _(i):
        pass_on(i, z, start)

    def sides(s, act):
        @pl.when(z - s >= 0)
        def _():
            act(z - s)

        @pl.when(z + s < cols)
        def _():
            act(z + s)

    @pl.loop(1, cols)
    def _(s):
        def act(c):
            arrive(k, z, c)
            ship_on(c, start)
            pass_on(z, c, start)

        sides(s, act)

    @pl.loop(0, cols)
    def _(i):
        @pl.when(i != z)
        def _():
            @pl.loop(1, cols)
            def _(s):
                def act(c):
                    arrive(k, i, c)
                    pass_on(i, c, start)

                sides(s, act)

    def scale(way, source):
        @pl.loop(0, cols)
        def _(c):
            wgt[way, c] = (source(c).astype(jnp.float32) * occ_ref[c]).astype(jnp.bfloat16)

    for way, present in ((0, has_down), (1, has_up)):

        @pl.when(present)
        def _():
            @pl.loop(0, cols)
            def _(c):
                remote(wgt.at[way, c], wgt.at[way, c], dsem.at[0], usem.at[way, c], (row, z)).wait_recv()

            scale(way, lambda c: wgt[way, c])

    scale(2, lambda c: gat[k, z, c])
    for d in range(1, per):
        kk = lax.rem(k + d, per)

        @pl.loop(0, cols)
        def _(i):
            @pl.loop(0, cols)
            def _(c):
                arrive(kk, i, c)

    def answer(t):
        low = t < place
        other = jnp.where(low, t, t + 1)
        slot = jnp.where(low, size + other - place, other - place - size) + W - 1
        near = (slot >= 0) & (slot < 2 * W - 1)
        return low, other, slot, near

    def reply(t):
        low, other, slot, near = answer(t)
        there = lax.rem(jnp.where(low, row - per, row + per) + rows, rows)
        go = near & jnp.where(low, row - per >= 0, row + per < rows)
        slot = jnp.clip(slot, 0, 2 * W - 2)
        return go, remote(res.at[t], out_ref.at[slot], osem.at[t], qsem.at[slot], (there, z))

    def local(t):
        other = t - (size - 1)
        slot = other - place + W - 1
        near = (slot >= 0) & (slot < 2 * W - 1)
        slot = jnp.clip(slot, 0, 2 * W - 2)
        return near, pltpu.make_async_copy(res.at[t], out_ref.at[slot], osem.at[t])

    def product(t, way, other):
        kk, i = other // cols, lax.rem(other, cols)
        total = jnp.zeros(res.shape[1:], jnp.float32)
        for c in range(cols):
            total = total + lax.dot_general(
                wgt[way, c], gat[kk, i, c], (((1,), (1,)), ((), ())), preferred_element_type=jnp.float32
            )
        res[t] = total.astype(jnp.bfloat16)

    @pl.loop(0, size - 1)
    def _(t):
        go, copy = reply(t)
        low, other, _, _ = answer(t)

        @pl.when(go)
        def _():
            product(t, jnp.where(low, 0, 1), other)
            copy.start()

    @pl.loop(size - 1, 2 * size - 1)
    def _(t):
        near, copy = local(t)

        @pl.when(near)
        def _():
            product(t, 2, t - (size - 1))
            copy.start()

    for d in range(1, cols):
        direct(lax.rem(z + d, cols)).wait_send()

    @pl.loop(0, cols)
    def _(c):
        ship_on(c, sent)

        @pl.loop(0, cols)
        def _(i):
            pass_on(i, c, sent)

    @pl.loop(0, size - 1)
    def _(t):
        go, copy = reply(t)

        @pl.when(go)
        def _():
            copy.wait_send()

        low, other, slot, near = answer(t)
        due = near & jnp.where(low, row + per < rows, row - per >= 0)
        slot = jnp.clip(slot, 0, 2 * W - 2)

        @pl.when(due)
        def _():
            remote(res.at[t], out_ref.at[slot], osem.at[t], qsem.at[slot], (row, z)).wait_recv()

    @pl.loop(size - 1, 2 * size - 1)
    def _(t):
        near, copy = local(t)

        @pl.when(near)
        def _():
            copy.wait()


def shards(coeffs, occupations, block_order, neighbours, counts):
    rows, cols = lax.axis_size("row"), lax.axis_size("col")
    states = coeffs.shape[1]
    depth = coeffs.shape[0] // cols
    per = -(-W // cols)
    size = per * cols
    slots_total = 2 * W - 1
    first = lax.axis_index("row") * cols
    picks = lax.dynamic_slice_in_dim(block_order, first, cols) - first
    own = coeffs.reshape(cols, depth, states)[picks]
    occ = occupations.reshape(cols, 1, states)
    dma = pltpu.SemaphoreType.DMA
    blocks = pl.pallas_call(
        functools.partial(kernel, rows, cols, per),
        out_shape=jax.ShapeDtypeStruct((slots_total, depth, depth), jnp.bfloat16),
        in_specs=[pl.BlockSpec(memory_space=pl.ANY), pl.BlockSpec(memory_space=pltpu.VMEM)],
        out_specs=pl.BlockSpec(memory_space=pl.ANY),
        scratch_shapes=[
            pltpu.VMEM((per, cols, cols, depth, states), jnp.bfloat16),
            pltpu.VMEM((3, cols, depth, states), jnp.bfloat16),
            pltpu.VMEM((2 * size - 1, depth, depth), jnp.bfloat16),
            dma,
            dma((cols,)),
            dma((2, cols, cols)),
            dma((max(per - 1, 1), cols, cols)),
            dma((per, cols, cols)),
            dma((2, cols)),
            dma((2, cols)),
            dma((2 * size - 1,)),
            dma((slots_total,)),
        ],
        compiler_params=pltpu.CompilerParams(
            collective_id=0, has_side_effects=True, vmem_limit_bytes=60 * 1024 * 1024
        ),
        name="density_blocks",
    )(own, occ)
    here = first + lax.axis_index("col")
    offsets = neighbours[0] - here + (W - 1)
    live = jnp.arange(neighbours.shape[1], dtype=jnp.int32) < counts[0]
    return jnp.where(live[:, None, None], blocks[offsets], 0)[None]


def solution(mesh):
    return jax.shard_map(
        shards,
        mesh=mesh,
        in_specs=(P("row", "col"), P(), P(), P(("row", "col"), None), P(("row", "col"))),
        out_specs=P(("row", "col"), None, None, None),
        check_vma=False,
    )
```

time: 821 us -> 258 us (0.31)
  the two profiles are of different devices: /device:TPU:20 before, /device:TPU:5 now
where the time goes in v1:
time: 258 us; the launch traced here: 257 us
  Pallas kernels  238 us (92%)
  local copies, waits for them, and re-layouts  10.7 us (4%)
  other arithmetic  7.94 us (3%)
    pallas_call x1, Pallas kernels, shards(): pl.pallas_call(functools.partial(kernel, rows, cols, per), out_shape=jax....  238 us
    gather x1, local copies, waits for them, and re-layouts, shards(): return jnp.where(live[:, None, None], blocks[offsets], 0)[None]  7.96 us
    select_n x2, other arithmetic, shards(): return jnp.where(live[:, None, None], blocks[offsets], 0)[None]  7.04 us

profile of v1, /device:TPU:5, one launch (start us, length us, event | category | flops | bytes accessed | tf_op | source)
XLA Modules:
  0.0 257.3 jit_solution(6446863430977685291)
XLA Ops:
  0.0 0.0 copy-start
  0.0 0.0 copy-start.1
  0.0 0.9 compare_select_fusion.1
  0.9 0.7 copy-done
  1.6 2.0 gather_fusion
  3.6 238.0 %density_blocks.1 = bf16[15,512,512]{2,1,0:T(8,128)(2,1)} custom-call(bf16[4,512,512]{2,1,0:T(8,128)(2,1)} %gather_fusion, f32[4,1,512]{2,1,0:T(1,128)} %bitcast.13), custom_call_target="tpu_custom_call" | custom-call | tf_op jit(solution)/shard_map/density_blocks/pallas_call | solution.py:252
  241.6 0.0 copy-done.1
  241.6 8.0 %gather_fusion.1 = bf16[15,512,512]{2,1,0:T(8,128)(2,1)} fusion(bf16[15,512,512]{2,1,0:T(8,128)(2,1)} %density_blocks.1, s32[1024]{0:T(1024)S(1)} %pad_clamp_fusion), kind=kCustom, calls=%fused_computation.1 | custom fusion | bytes 15728700 | tf_op jit(solution)/shard_map/gather | solution.py:279
  250.2 7.0 %bitcast_select_fusion = bf16[1,15,512,512]{3,2,1,0:T(8,128)(2,1)} fusion(bf16[15,512,512]{2,1,0:T(8,128)(2,1)} %gather_fusion.1, pred[15]{0:T(512)(128)(4,1)S(1)} %iota_compare_fusion), kind=kLoop, calls=%fused_computation.2 | loop fusion | flops 3932160 | bytes 15728655 | tf_op jit(solution)/shard_map/jit(_where)/select_n | solution.py:279
  (4 shorter events, 0.0 us)
Async XLA Ops:
  0.0 1.6 copy-start
  0.0 241.6 %copy-start.1 = (s32[1,15]{1,0:T(1,128)S(1)}, s32[1,15]{1,0:T(1,128)}, u32[]{:S(2)}) copy-start(s32[1,15]{1,0:T(1,128)} %param.8) | copy-start | bytes 184

commit v2 on v1

--- a/solution.py
+++ b/solution.py
@@ -8,16 +8,25 @@
 from jax.sharding import PartitionSpec as P
 
 W = 8
+LAG = 2
 MESH = pl.DeviceIdType.MESH
 
 
-def kernel(rows, cols, per, own_ref, occ_ref, out_ref, gat, wgt, res, in_sem, dsem, fsem, psem, rsem, xsem, usem, osem, qsem):
+def kernel(rows, cols, per, own_ref, occ_ref, out_ref, gat, raw, wgt, res, in_sem, dsem, fsem, psem, rsem, xsem, ysem, usem, osem, qsem):
     row, z = lax.axis_index("row"), lax.axis_index("col")
     k = lax.rem(row, per)
     base = row - k
     place = k * cols + z
     size = per * cols
     has_up, has_down = row + per < rows, row >= per
+    has_up2, has_down2 = row + 2 * per < rows, row >= 2 * per
+    odd = lax.rem(row // per, 2) == 1
+    ships_up = has_up & jnp.logical_not(odd) & ((place > 0) | has_down)
+    ships_down = has_down & jnp.where(odd, (place < size - 1) | has_up, (place < size - 1) & jnp.logical_not(has_up))
+    relays_up = has_up2 & (place > 0) & jnp.logical_not(odd)
+    relays_down = has_down2 & (place < size - 1) & odd
+    lower, upper = has_down & (place > 0), has_up & (place < size - 1)
+    edge = (z == 0) | (z == cols - 1)
 
     def remote(src, dst, send, recv, device):
         return pltpu.make_async_remote_copy(
@@ -38,7 +47,14 @@
 
     def ship(way, c):
         there = lax.rem(row + (1 - 2 * way) * per + rows, rows)
-        return remote(gat.at[k, z, c], wgt.at[way, c], xsem.at[way, c], usem.at[way, c], (there, z))
+        return remote(gat.at[k, z, c], raw.at[way, c], xsem.at[way, c], usem.at[way, c], (there, z))
+
+    def relay(way, c):
+        there = lax.rem(row + (2 - 4 * way) * per + 2 * rows, rows)
+        return remote(raw.at[1 - way, c], raw.at[way, c], ysem.at[c], usem.at[way, c], (there, z))
+
+    def taken(way, c):
+        remote(raw.at[way, c], raw.at[way, c], xsem.at[0, 0], usem.at[way, c], (row, z)).wait_recv()
 
     def arrive(kk, i, c):
         remote(gat.at[kk, i, c], gat.at[kk, i, c], dsem.at[0], rsem.at[kk, i, c], (row, z)).wait_recv()
@@ -56,11 +72,11 @@
             act(partner(d, i, c))
 
     def ship_on(c, act):
-        @pl.when(has_up)
+        @pl.when(ships_up)
         def _():
             act(ship(0, c))
 
-        @pl.when(has_down)
+        @pl.when(ships_down)
         def _():
             act(ship(1, c))
 
@@ -78,15 +94,16 @@
     for d in range(1, per):
         pl.semaphore_signal(barrier, inc=1, device_id=(base + lax.rem(k + d, per), z), device_id_type=MESH)
 
-    @pl.when(has_up)
-    def _():
-        pl.semaphore_signal(barrier, inc=1, device_id=(lax.rem(row + per, rows), z), device_id_type=MESH)
-
-    @pl.when(has_down)
-    def _():
-        pl.semaphore_signal(barrier, inc=1, device_id=(lax.rem(row - per + rows, rows), z), device_id_type=MESH)
-
-    pl.semaphore_wait(barrier, cols + per - 2 + has_up.astype(jnp.int32) + has_down.astype(jnp.int32))
+    greeted = cols + per - 2
+    for present, step in ((has_up, per), (has_down, -per), (has_up2, 2 * per), (has_down2, -2 * per)):
+        greeted = greeted + present.astype(jnp.int32)
+
+        @pl.when(present)
+        def _():
+            there = lax.rem(row + step + 2 * rows, rows)
+            pl.semaphore_signal(barrier, inc=1, device_id=(there, z), device_id_type=MESH)
+
+    pl.semaphore_wait(barrier, greeted)
     fill.wait()
 
     for d in range(1, cols):
@@ -115,42 +132,47 @@
 
         sides(s, act)
 
-    @pl.loop(0, cols)
-    def _(i):
-        @pl.when(i != z)
-        def _():
-            @pl.loop(1, cols)
-            def _(s):
-                def act(c):
-                    arrive(k, i, c)
-                    pass_on(i, c, start)
-
-                sides(s, act)
+    def relay_on(c, act):
+        @pl.when(relays_up)
+        def _():
+            act(relay(0, c), 1)
+
+        @pl.when(relays_down)
+        def _():
+            act(relay(1, c), 0)
+
+    def receive_and_relay(c):
+        def act(copy, way):
+            taken(way, c)
+            copy.start()
+
+        relay_on(c, act)
+
+    receive_and_relay(z)
+
+    @pl.loop(1, cols)
+    def _(s):
+        sides(s, receive_and_relay)
 
     def scale(way, source):
         @pl.loop(0, cols)
         def _(c):
             wgt[way, c] = (source(c).astype(jnp.float32) * occ_ref[c]).astype(jnp.bfloat16)
 
-    for way, present in ((0, has_down), (1, has_up)):
-
-        @pl.when(present)
-        def _():
-            @pl.loop(0, cols)
-            def _(c):
-                remote(wgt.at[way, c], wgt.at[way, c], dsem.at[0], usem.at[way, c], (row, z)).wait_recv()
-
-            scale(way, lambda c: wgt[way, c])
-
-    scale(2, lambda c: gat[k, z, c])
-    for d in range(1, per):
-        kk = lax.rem(k + d, per)
-
-        @pl.loop(0, cols)
-        def _(i):
-            @pl.loop(0, cols)
-            def _(c):
-                arrive(kk, i, c)
+    def prepare():
+        for way, present, waited in ((0, lower, relays_down), (1, upper, relays_up)):
+
+            @pl.when(present)
+            def _():
+                @pl.when(jnp.logical_not(waited))
+                def _():
+                    @pl.loop(0, cols)
+                    def _(c):
+                        taken(way, c)
+
+                scale(way, lambda c: raw[way, c])
+
+        scale(2, lambda c: gat[k, z, c])
 
     def answer(t):
         low = t < place
@@ -182,15 +204,103 @@
             )
         res[t] = total.astype(jnp.bfloat16)
 
+    def home(other):
+        t = other + size - 1
+        near, copy = local(t)
+
+        @pl.when(near)
+        def _():
+            product(t, 2, other)
+            copy.start()
+
+    def away(other):
+        low = other < place
+        t = jnp.clip(jnp.where(low, other, other - 1), 0, size - 2)
+        go, copy = reply(t)
+
+        @pl.when(go & (other != place))
+        def _():
+            product(t, jnp.where(low, 0, 1), other)
+            copy.start()
+
+    def work(q):
+        i = jnp.where(q == 0, z, jnp.where(q - 1 < z, q - 1, q))
+        for d in range(1, per):
+            kk = lax.rem(k + d, per)
+
+            @pl.loop(0, cols)
+            def _(c):
+                arrive(kk, i, c)
+
+        @pl.loop(0, per)
+        def _(kk):
+            away(kk * cols + i)
+
+        @pl.when(edge)
+        def _():
+            @pl.loop(0, per)
+            def _(kk):
+                home(kk * cols + i)
+
+    lag = jnp.where(edge, 0, LAG)
+
+    @pl.loop(0, cols + LAG)
+    def _(n):
+        @pl.when((n >= 1) & (n < cols))
+        def _():
+            i = jnp.where(n - 1 < z, n - 1, n)
+
+            @pl.loop(1, cols)
+            def _(s):
+                def act(c):
+                    arrive(k, i, c)
+                    pass_on(i, c, start)
+
+                sides(s, act)
+
+        q = n - lag
+
+        @pl.when(q == 0)
+        def _():
+            prepare()
+
+        @pl.when((q >= 0) & (q < cols))
+        def _():
+            work(q)
+
+    @pl.when(jnp.logical_not(edge))
+    def _():
+        @pl.loop(0, size)
+        def _(other):
+            home(other)
+
+    for d in range(1, cols):
+        direct(lax.rem(z + d, cols)).wait_send()
+
+    @pl.loop(0, cols)
+    def _(c):
+        ship_on(c, sent)
+        relay_on(c, lambda copy, way: sent(copy))
+
+        @pl.loop(0, cols)
+        def _(i):
+            pass_on(i, c, sent)
+
     @pl.loop(0, size - 1)
     def _(t):
         go, copy = reply(t)
-        low, other, _, _ = answer(t)
 
         @pl.when(go)
         def _():
-            product(t, jnp.where(low, 0, 1), other)
-            copy.start()
+            copy.wait_send()
+
+        low, other, slot, near = answer(t)
+        due = near & jnp.where(low, row + per < rows, row - per >= 0)
+        slot = jnp.clip(slot, 0, 2 * W - 2)
+
+        @pl.when(due)
+        def _():
+            remote(res.at[t], out_ref.at[slot], osem.at[t], qsem.at[slot], (row, z)).wait_recv()
 
     @pl.loop(size - 1, 2 * size - 1)
     def _(t):
@@ -198,43 +308,19 @@
 
         @pl.when(near)
         def _():
-            product(t, 2, t - (size - 1))
-            copy.start()
-
-    for d in range(1, cols):
-        direct(lax.rem(z + d, cols)).wait_send()
-
-    @pl.loop(0, cols)
-    def _(c):
-        ship_on(c, sent)
-
-        @pl.loop(0, cols)
-        def _(i):
-            pass_on(i, c, sent)
-
-    @pl.loop(0, size - 1)
-    def _(t):
-        go, copy = reply(t)
-
-        @pl.when(go)
-        def _():
-            copy.wait_send()
-
-        low, other, slot, near = answer(t)
-        due = near & jnp.where(low, row + per < rows, row - per >= 0)
-        slot = jnp.clip(slot, 0, 2 * W - 2)
-
-        @pl.when(due)
-        def _():
-            remote(res.at[t], out_ref.at[slot], osem.at[t], qsem.at[slot], (row, z)).wait_recv()
-
-    @pl.loop(size - 1, 2 * size - 1)
-    def _(t):
-        near, copy = local(t)
-
-        @pl.when(near)
-        def _():
             copy.wait()
+
+
+def place_blocks(at_ref, live_ref, block_ref, out_ref):
+    live = live_ref[pl.program_id(0)] > 0
+
+    @pl.when(live)
+    def _():
+        out_ref[...] = block_ref[...]
+
+    @pl.when(jnp.logical_not(live))
+    def _():
+        out_ref[...] = jnp.zeros_like(out_ref)
 
 
 def shards(coeffs, occupations, block_order, neighbours, counts):
@@ -256,6 +342,7 @@
         out_specs=pl.BlockSpec(memory_space=pl.ANY),
         scratch_shapes=[
             pltpu.VMEM((per, cols, cols, depth, states), jnp.bfloat16),
+            pltpu.VMEM((2, cols, depth, states), jnp.bfloat16),
             pltpu.VMEM((3, cols, depth, states), jnp.bfloat16),
             pltpu.VMEM((2 * size - 1, depth, depth), jnp.bfloat16),
             dma,
@@ -264,6 +351,7 @@
             dma((max(per - 1, 1), cols, cols)),
             dma((per, cols, cols)),
             dma((2, cols)),
+            dma((cols,)),
             dma((2, cols)),
             dma((2 * size - 1,)),
             dma((slots_total,)),
@@ -276,7 +364,18 @@
     here = first + lax.axis_index("col")
     offsets = neighbours[0] - here + (W - 1)
     live = jnp.arange(neighbours.shape[1], dtype=jnp.int32) < counts[0]
-    return jnp.where(live[:, None, None], blocks[offsets], 0)[None]
+    plan = pltpu.PrefetchScalarGridSpec(
+        num_scalar_prefetch=2,
+        grid=(offsets.shape[0],),
+        in_specs=[pl.BlockSpec((1, depth, depth), lambda j, at, live: (at[j], 0, 0))],
+        out_specs=pl.BlockSpec((1, depth, depth), lambda j, at, live: (j, 0, 0)),
+    )
+    return pl.pallas_call(
+        place_blocks,
+        grid_spec=plan,
+        out_shape=jax.ShapeDtypeStruct((offsets.shape[0], depth, depth), jnp.bfloat16),
+        name="place_blocks",
+    )(offsets, live.astype(jnp.int32), blocks)[None]
 
 
 def solution(mesh):

time: 258 us -> 209 us (0.81)
  the two profiles are of different devices: /device:TPU:5 before, /device:TPU:20 now
where the time goes in v2:
time: 209 us; the launch traced here: 206 us
  Pallas kernels  201 us (96%)
  other arithmetic  2.41 us (1%)
    pallas_call x1, Pallas kernels, shards(): pl.pallas_call(functools.partial(kernel, rows, cols, per), out_shape=jax....  191 us
    pallas_call x1, Pallas kernels, shards(): pl.pallas_call(place_blocks, grid_spec=plan, out_shape=jax.ShapeDtypeStru...  9.51 us

profile of v2, /device:TPU:20, one launch (start us, length us, event | category | flops | bytes accessed | tf_op | source)
XLA Modules:
  0.0 205.8 jit_solution(17121997255891465879)
XLA Ops:
  0.0 0.0 copy-start
  0.8 0.5 compare_convert_fusion.live_ref
  1.3 1.2 add_bitcast_fusion.at_ref
  2.5 0.7 compare_select_fusion
  3.2 0.0 copy-done
  3.2 2.0 gather_fusion
  5.2 191.1 %density_blocks.1.block_ref = bf16[15,512,512]{2,1,0:T(8,128)(2,1)} custom-call(bf16[4,512,512]{2,1,0:T(8,128)(2,1)} %gather_fusion, f32[4,1,512]{2,1,0:T(1,128)} %bitcast.8), custom_call_target="tpu_custom_call" | custom-call | tf_op jit(solution)/shard_map/density_blocks/pallas_call | solution.py:338
  196.3 9.5 %place_blocks.1 = bf16[15,512,512]{2,1,0:T(8,128)(2,1)} custom-call(s32[15]{0:T(128)} %add_bitcast_fusion.at_ref, s32[15]{0:T(128)} %compare_convert_fusion.live_ref, bf16[15,512,512]{2,1,0:T(8,128)(2,1)} %density_blocks.1.block_ref), custom_call_target="tpu_custom_call" | custom-call | tf_op jit(solution)/shard_map/place_blocks/pallas_call | solution.py:373
  (1 shorter events, 0.0 us)
Async XLA Ops:
  0.0 3.2 %copy-start = (bf16[2048,512]{1,0:T(8,128)(2,1)S(1)}, bf16[2048,512]{1,0:T(8,128)(2,1)}, u32[]{:S(2)}) copy-start(bf16[2048,512]{1,0:T(8,128)(2,1)} %param.5) | copy-start | bytes 6291460

commit v3 on v2

--- a/solution.py
+++ b/solution.py
@@ -8,11 +8,10 @@
 from jax.sharding import PartitionSpec as P
 
 W = 8
-LAG = 2
 MESH = pl.DeviceIdType.MESH
 
 
-def kernel(rows, cols, per, own_ref, occ_ref, out_ref, gat, raw, wgt, res, in_sem, dsem, fsem, psem, rsem, xsem, ysem, usem, osem, qsem):
+def kernel(rows, cols, per, own_ref, occ_ref, out_ref, gat, raw, wgt, res, in_sem, fsem, psem, rsem, xsem, ysem, usem, osem, qsem):
     row, z = lax.axis_index("row"), lax.axis_index("col")
     k = lax.rem(row, per)
     base = row - k
@@ -33,9 +32,6 @@
             src_ref=src, dst_ref=dst, send_sem=send, recv_sem=recv, device_id=device, device_id_type=MESH
         )
 
-    def direct(i):
-        return remote(gat.at[k, i, z], gat.at[k, i, z], dsem.at[i], rsem.at[k, i, z], (row, i))
-
     def onward(way, i, c):
         step = 1 - 2 * way
         there = lax.rem(z + step + cols, cols)
@@ -57,17 +53,14 @@
         remote(raw.at[way, c], raw.at[way, c], xsem.at[0, 0], usem.at[way, c], (row, z)).wait_recv()
 
     def arrive(kk, i, c):
-        remote(gat.at[kk, i, c], gat.at[kk, i, c], dsem.at[0], rsem.at[kk, i, c], (row, z)).wait_recv()
-
-    def pass_on(i, c, act):
-        @pl.when((c <= z) & (z < cols - 1) & (i != z + 1))
-        def _():
-            act(onward(0, i, c))
-
-        @pl.when((c >= z) & (z > 0) & (i != z - 1))
-        def _():
-            act(onward(1, i, c))
-
+        remote(gat.at[kk, i, c], gat.at[kk, i, c], psem.at[0, 0, 0], rsem.at[kk, i, c], (row, z)).wait_recv()
+
+    def onward_on(way, i, c, act):
+        @pl.when(jnp.where(way == 0, (c <= z) & (z < cols - 1), (c >= z) & (z > 0)))
+        def _():
+            act(onward(way, i, c))
+
+    def partner_on(i, c, act):
         for d in range(1, per):
             act(partner(d, i, c))
 
@@ -106,31 +99,30 @@
     pl.semaphore_wait(barrier, greeted)
     fill.wait()
 
-    for d in range(1, cols):
-        direct(lax.rem(z + d, cols)).start()
-    ship_on(z, start)
-
-    @pl.loop(0, cols)
-    def _(i):
-        pass_on(i, z, start)
-
-    def sides(s, act):
-        @pl.when(z - s >= 0)
-        def _():
-            act(z - s)
-
-        @pl.when(z + s < cols)
-        def _():
-            act(z + s)
-
-    @pl.loop(1, cols)
-    def _(s):
-        def act(c):
-            arrive(k, z, c)
-            ship_on(c, start)
-            pass_on(z, c, start)
-
-        sides(s, act)
+    def stream(way, i, s):
+        c = z - s if way == 0 else z + s
+
+        @pl.when((c >= 0) & (c < cols))
+        def _():
+            @pl.when(s > 0)
+            def _():
+                arrive(k, i, c)
+
+            onward_on(way, i, c, start)
+
+            @pl.when(s > 0)
+            def _():
+                @pl.when(i == z)
+                def _():
+                    ship_on(c, start)
+
+                partner_on(i, c, start)
+
+    def step(n):
+        @pl.loop(0, cols)
+        def _(s):
+            stream(0, cols - 1 - n, s)
+            stream(1, n, s)
 
     def relay_on(c, act):
         @pl.when(relays_up)
@@ -148,11 +140,18 @@
 
         relay_on(c, act)
 
-    receive_and_relay(z)
-
-    @pl.loop(1, cols)
-    def _(s):
-        sides(s, receive_and_relay)
+    def relay_all():
+        receive_and_relay(z)
+
+        @pl.loop(1, cols)
+        def _(s):
+            @pl.when(z - s >= 0)
+            def _():
+                receive_and_relay(z - s)
+
+            @pl.when(z + s < cols)
+            def _():
+                receive_and_relay(z + s)
 
     def scale(way, source):
         @pl.loop(0, cols)
@@ -223,8 +222,7 @@
             product(t, jnp.where(low, 0, 1), other)
             copy.start()
 
-    def work(q):
-        i = jnp.where(q == 0, z, jnp.where(q - 1 < z, q - 1, q))
+    def work(i):
         for d in range(1, per):
             kk = lax.rem(k + d, per)
 
@@ -242,31 +240,38 @@
             def _(kk):
                 home(kk * cols + i)
 
-    lag = jnp.where(edge, 0, LAG)
-
-    @pl.loop(0, cols + LAG)
+    relay_at = jnp.where(edge, 0, jnp.maximum(z, cols - 1 - z))
+    ready_at = jnp.where(edge, 0, cols - 1)
+
+    ship_on(z, start)
+
+    @pl.loop(0, cols)
     def _(n):
-        @pl.when((n >= 1) & (n < cols))
-        def _():
-            i = jnp.where(n - 1 < z, n - 1, n)
-
-            @pl.loop(1, cols)
-            def _(s):
-                def act(c):
-                    arrive(k, i, c)
-                    pass_on(i, c, start)
-
-                sides(s, act)
-
-        q = n - lag
-
-        @pl.when(q == 0)
+        step(n)
+
+        @pl.when(n == 0)
+        def _():
+            @pl.loop(0, cols)
+            def _(i):
+                partner_on(i, z, start)
+
+        @pl.when(n == relay_at)
+        def _():
+            relay_all()
+
+        @pl.when(n == ready_at)
         def _():
             prepare()
 
-        @pl.when((q >= 0) & (q < cols))
-        def _():
-            work(q)
+        @pl.when(n >= ready_at)
+        def _():
+            @pl.loop(0, cols)
+            def _(i):
+                whole = jnp.where(z == 0, i, jnp.where(z == cols - 1, cols - 1 - i, jnp.maximum(i, cols - 1 - i)))
+
+                @pl.when((whole == n) | ((n == ready_at) & (whole < n)))
+                def _():
+                    work(i)
 
     @pl.when(jnp.logical_not(edge))
     def _():
@@ -274,9 +279,6 @@
         def _(other):
             home(other)
 
-    for d in range(1, cols):
-        direct(lax.rem(z + d, cols)).wait_send()
-
     @pl.loop(0, cols)
     def _(c):
         ship_on(c, sent)
@@ -284,7 +286,9 @@
 
         @pl.loop(0, cols)
         def _(i):
-            pass_on(i, c, sent)
+            onward_on(0, i, c, sent)
+            onward_on(1, i, c, sent)
+            partner_on(i, c, sent)
 
     @pl.loop(0, size - 1)
     def _(t):
@@ -311,16 +315,37 @@
             copy.wait()
 
 
-def place_blocks(at_ref, live_ref, block_ref, out_ref):
-    live = live_ref[pl.program_id(0)] > 0
-
-    @pl.when(live)
-    def _():
-        out_ref[...] = block_ref[...]
-
-    @pl.when(jnp.logical_not(live))
-    def _():
-        out_ref[...] = jnp.zeros_like(out_ref)
+def place_blocks(neighbours_ref, counts_ref, block_ref, out_ref, held, blank, in_sem, out_sem):
+    here = lax.axis_index("row") * lax.axis_size("col") + lax.axis_index("col")
+    blank[...] = jnp.zeros_like(blank)
+
+    def fetch(j):
+        at = jnp.clip(neighbours_ref[0, j] - here + (W - 1), 0, 2 * W - 2)
+        return pltpu.make_async_copy(block_ref.at[at], held.at[j], in_sem.at[j])
+
+    def store(j, source):
+        return pltpu.make_async_copy(source, out_ref.at[j], out_sem.at[j])
+
+    slots = out_ref.shape[0]
+    for j in range(slots):
+
+        @pl.when(j < counts_ref[0])
+        def _():
+            fetch(j).start()
+
+        @pl.when(j >= counts_ref[0])
+        def _():
+            store(j, blank).start()
+
+    for j in range(slots):
+
+        @pl.when(j < counts_ref[0])
+        def _():
+            fetch(j).wait()
+            store(j, held.at[j]).start()
+
+    for j in range(slots):
+        store(j, blank).wait()
 
 
 def shards(coeffs, occupations, block_order, neighbours, counts):
@@ -346,7 +371,6 @@
             pltpu.VMEM((3, cols, depth, states), jnp.bfloat16),
             pltpu.VMEM((2 * size - 1, depth, depth), jnp.bfloat16),
             dma,
-            dma((cols,)),
             dma((2, cols, cols)),
             dma((max(per - 1, 1), cols, cols)),
             dma((per, cols, cols)),
@@ -361,21 +385,25 @@
         ),
         name="density_blocks",
     )(own, occ)
-    here = first + lax.axis_index("col")
-    offsets = neighbours[0] - here + (W - 1)
-    live = jnp.arange(neighbours.shape[1], dtype=jnp.int32) < counts[0]
-    plan = pltpu.PrefetchScalarGridSpec(
-        num_scalar_prefetch=2,
-        grid=(offsets.shape[0],),
-        in_specs=[pl.BlockSpec((1, depth, depth), lambda j, at, live: (at[j], 0, 0))],
-        out_specs=pl.BlockSpec((1, depth, depth), lambda j, at, live: (j, 0, 0)),
-    )
-    return pl.pallas_call(
+    slots = neighbours.shape[1]
+    placed = pl.pallas_call(
         place_blocks,
-        grid_spec=plan,
-        out_shape=jax.ShapeDtypeStruct((offsets.shape[0], depth, depth), jnp.bfloat16),
+        out_shape=jax.ShapeDtypeStruct((slots, depth, depth), jnp.bfloat16),
+        in_specs=[
+            pl.BlockSpec(memory_space=pltpu.SMEM),
+            pl.BlockSpec(memory_space=pltpu.SMEM),
+            pl.BlockSpec(memory_space=pl.ANY),
+        ],
+        out_specs=pl.BlockSpec(memory_space=pl.ANY),
+        scratch_shapes=[
+            pltpu.VMEM((slots, depth, depth), jnp.bfloat16),
+            pltpu.VMEM((depth, depth), jnp.bfloat16),
+            dma((slots,)),
+            dma((slots,)),
+        ],
         name="place_blocks",
-    )(offsets, live.astype(jnp.int32), blocks)[None]
+    )(neighbours, counts, blocks)
+    return placed[None]
 
 
 def solution(mesh):

time: 209 us -> 305 us (1.46)
  Pallas kernels: 201 us -> 301 us
    pallas_call x1, Pallas kernels: 191 us -> 294 us  [shards(): pl.pallas_call(functools.partial(kernel, rows, cols, per), out_shape=jax....]
where the time goes in v3:
time: 305 us
  Pallas kernels  301 us (99%)
    pallas_call x1, Pallas kernels, shards(): pl.pallas_call(functools.partial(kernel, rows, cols, per), out_shape=jax....  294 us
    pallas_call x1, Pallas kernels, shards(): pl.pallas_call(place_blocks, out_shape=jax.ShapeDtypeStruct((slots, depth...  6.87 us

profile of v3, /device:TPU:20, one launch (start us, length us, event | category | flops | bytes accessed | tf_op | source)
XLA Modules:
  0.0 304.7 jit_solution(12894103930349660855)
XLA Ops:
  0.0 0.0 copy-start
  0.8 0.7 compare_select_fusion
  1.5 0.1 copy-done
  1.6 2.0 gather_fusion
  3.6 294.2 %density_blocks.1.block_ref = bf16[15,512,512]{2,1,0:T(8,128)(2,1)} custom-call(bf16[4,512,512]{2,1,0:T(8,128)(2,1)} %gather_fusion, f32[4,1,512]{2,1,0:T(1,128)} %bitcast.4), custom_call_target="tpu_custom_call" | custom-call | tf_op jit(solution)/shard_map/density_blocks/pallas_call | solution.py:363
  297.8 6.9 %place_blocks.1 = bf16[15,512,512]{2,1,0:T(8,128)(2,1)} custom-call(s32[1,15]{1,0:T(1,128)} %neighbours_ref.1, s32[1]{0:T(128)S(6)} %copy.6.counts_ref, bf16[15,512,512]{2,1,0:T(8,128)(2,1)} %density_blocks.1.block_ref), custom_call_target="tpu_custom_call" | custom-call | tf_op jit(solution)/shard_map/place_blocks/pallas_call | solution.py:389
  (1 shorter events, 0.0 us)
Async XLA Ops:
  0.0 1.6 copy-start

commit v4 on v2

--- a/solution.py
+++ b/solution.py
@@ -8,7 +8,7 @@
 from jax.sharding import PartitionSpec as P
 
 W = 8
-LAG = 2
+LAG = 1
 MESH = pl.DeviceIdType.MESH
 
 
@@ -311,16 +311,37 @@
             copy.wait()
 
 
-def place_blocks(at_ref, live_ref, block_ref, out_ref):
-    live = live_ref[pl.program_id(0)] > 0
-
-    @pl.when(live)
-    def _():
-        out_ref[...] = block_ref[...]
-
-    @pl.when(jnp.logical_not(live))
-    def _():
-        out_ref[...] = jnp.zeros_like(out_ref)
+def place_blocks(neighbours_ref, counts_ref, block_ref, out_ref, held, blank, in_sem, out_sem):
+    here = lax.axis_index("row") * lax.axis_size("col") + lax.axis_index("col")
+    blank[...] = jnp.zeros_like(blank)
+
+    def fetch(j):
+        at = jnp.clip(neighbours_ref[0, j] - here + (W - 1), 0, 2 * W - 2)
+        return pltpu.make_async_copy(block_ref.at[at], held.at[j], in_sem.at[j])
+
+    def store(j, source):
+        return pltpu.make_async_copy(source, out_ref.at[j], out_sem.at[j])
+
+    slots = out_ref.shape[0]
+    for j in range(slots):
+
+        @pl.when(j < counts_ref[0])
+        def _():
+            fetch(j).start()
+
+        @pl.when(j >= counts_ref[0])
+        def _():
+            store(j, blank).start()
+
+    for j in range(slots):
+
+        @pl.when(j < counts_ref[0])
+        def _():
+            fetch(j).wait()
+            store(j, held.at[j]).start()
+
+    for j in range(slots):
+        store(j, blank).wait()
 
 
 def shards(coeffs, occupations, block_order, neighbours, counts):
@@ -361,21 +382,25 @@
         ),
         name="density_blocks",
     )(own, occ)
-    here = first + lax.axis_index("col")
-    offsets = neighbours[0] - here + (W - 1)
-    live = jnp.arange(neighbours.shape[1], dtype=jnp.int32) < counts[0]
-    plan = pltpu.PrefetchScalarGridSpec(
-        num_scalar_prefetch=2,
-        grid=(offsets.shape[0],),
-        in_specs=[pl.BlockSpec((1, depth, depth), lambda j, at, live: (at[j], 0, 0))],
-        out_specs=pl.BlockSpec((1, depth, depth), lambda j, at, live: (j, 0, 0)),
-    )
-    return pl.pallas_call(
+    slots = neighbours.shape[1]
+    placed = pl.pallas_call(
         place_blocks,
-        grid_spec=plan,
-        out_shape=jax.ShapeDtypeStruct((offsets.shape[0], depth, depth), jnp.bfloat16),
+        out_shape=jax.ShapeDtypeStruct((slots, depth, depth), jnp.bfloat16),
+        in_specs=[
+            pl.BlockSpec(memory_space=pltpu.SMEM),
+            pl.BlockSpec(memory_space=pltpu.SMEM),
+            pl.BlockSpec(memory_space=pl.ANY),
+        ],
+        out_specs=pl.BlockSpec(memory_space=pl.ANY),
+        scratch_shapes=[
+            pltpu.VMEM((slots, depth, depth), jnp.bfloat16),
+            pltpu.VMEM((depth, depth), jnp.bfloat16),
+            dma((slots,)),
+            dma((slots,)),
+        ],
         name="place_blocks",
-    )(offsets, live.astype(jnp.int32), blocks)[None]
+    )(neighbours, counts, blocks)
+    return placed[None]
 
 
 def solution(mesh):

time: 209 us -> 202 us (0.967)
  Pallas kernels: 201 us -> 195 us
    pallas_call x1, Pallas kernels: 9.51 us -> 6.42 us  [shards(): pl.pallas_call(place_blocks, out_shape=jax.ShapeDtypeStruct((slots, depth...]
where the time goes in v4:
time: 202 us; the launch traced here: 199 us
  Pallas kernels  195 us (97%)
  local copies, waits for them, and re-layouts  2.07 us (1%)
    pallas_call x1, Pallas kernels, shards(): pl.pallas_call(functools.partial(kernel, rows, cols, per), out_shape=jax....  189 us
    pallas_call x1, Pallas kernels, shards(): pl.pallas_call(place_blocks, out_shape=jax.ShapeDtypeStruct((slots, depth...  6.42 us

profile of v4, /device:TPU:20, one launch (start us, length us, event | category | flops | bytes accessed | tf_op | source)
XLA Modules:
  0.0 199.0 jit_solution(5914283627674834813)
XLA Ops:
  0.0 0.0 copy-start
  0.8 0.7 compare_select_fusion
  1.5 0.1 copy-done
  1.6 2.0 %gather_fusion = bf16[4,512,512]{2,1,0:T(8,128)(2,1)} fusion(bf16[4,512,512]{2,1,0:T(8,128)(2,1)S(1)} %bitcast.3, s32[1024]{0:T(1024)S(1)} %pad_clamp_fusion), kind=kCustom, calls=%fused_computation | custom fusion | bytes 4194320 | tf_op jit(solution)/shard_map/gather | solution.py:356
  3.6 189.0 %density_blocks.1.block_ref = bf16[15,512,512]{2,1,0:T(8,128)(2,1)} custom-call(bf16[4,512,512]{2,1,0:T(8,128)(2,1)} %gather_fusion, f32[4,1,512]{2,1,0:T(1,128)} %bitcast.4), custom_call_target="tpu_custom_call" | custom-call | tf_op jit(solution)/shard_map/density_blocks/pallas_call | solution.py:359
  192.6 6.4 %place_blocks.1 = bf16[15,512,512]{2,1,0:T(8,128)(2,1)} custom-call(s32[1,15]{1,0:T(1,128)} %neighbours_ref.1, s32[1]{0:T(128)S(6)} %copy.6.counts_ref, bf16[15,512,512]{2,1,0:T(8,128)(2,1)} %density_blocks.1.block_ref), custom_call_target="tpu_custom_call" | custom-call | tf_op jit(solution)/shard_map/place_blocks/pallas_call | solution.py:386
  (1 shorter events, 0.0 us)
Async XLA Ops:
  0.0 1.6 copy-start
